TPU v7x, 32 devices: a whole 2x2x4 slice. The times are simulated.
32 devices in a mesh: grp: 4 (over z), inner: 8 (over y, x, core).
Axes of the slice: x: 2, y: 2, z: 4, core: 2. Of those that a mesh axis runs over, the one named last changes fastest.
Arguments:
- design: float32 [8, 4096, 1024], P('inner', 'grp'), may hold values from -6 to 6
- row_signs: int32 [8, 4096], P('inner', 'grp'), may hold values from 0 to 1
- kept_rows: int32 [8, 2048], P('inner'), may hold values from 0 to 4095, as said below
Outputs:
- factored: float32 [2048, 1024], P('grp')
Inputs may be any that keep to these rules, and one draw needn't show every extreme that they name: `kept_rows`: within each block the 2048 kept row numbers are distinct, and each block keeps its first and its last row.
All inputs are finite; a program needn't handle non-finite values.
Results may differ from a plain program's by a relative error of at most 0.0048.
Values may be sent and summed in bfloat16 or wider, within the bound.
No kernel may reach another device: no remote copies, remote signals or barrier semaphores. Data moves between devices by JAX's collectives and lax.ppermute only.
A program may use at most 64 MiB of HBM per device.

v0:
```python
import math
import jax
import jax.numpy as jnp
from jax import lax
from jax.sharding import PartitionSpec as P

COLS_DONE = 8
epsilon = 1e-06


def sign_table(row_ids, col_ids):
    common_bits = jnp.bitwise_and(row_ids[:, None], col_ids[None, :])
    ones_total = jnp.zeros(common_bits.shape, jnp.int32)
    for bit_pos in range(4):
        ones_total = ones_total + jnp.bitwise_and(jnp.right_shift(common_bits, bit_pos), 1)
    return 1.0 - 2.0 * jnp.bitwise_and(ones_total, 1).astype(jnp.float32)


def pick_rows(table_rows, chosen_rows):
    return jnp.take(table_rows, chosen_rows, axis=0)


def on_device(design, row_signs, kept_rows):
    block_count, local_rows, columns = design.shape
    keep_count = kept_rows.shape[1]
    groups = lax.axis_size("grp")
    owned_rows = keep_count // groups
    highest = lax.Precision.HIGHEST
    sixteen = jnp.arange(16, dtype=jnp.int32)
    hadamard = sign_table(sixteen, sixteen).astype(jnp.bfloat16)
    flipped = (design * (1 - 2 * row_signs).astype(jnp.float32)[:, :, None]).astype(jnp.bfloat16)
    lowest = flipped.reshape(block_count * local_rows // 16, 16, columns)
    first_pass = jnp.einsum(
        "hc,ncd->nhd", hadamard, lowest, preferred_element_type=jnp.float32
    ).astype(jnp.bfloat16)
    middle_view = first_pass.reshape(block_count * local_rows // 256, 16, 16, columns)
    second_pass = jnp.einsum(
        "hb,mbcd->mhcd", hadamard, middle_view, preferred_element_type=jnp.float32
    ).astype(jnp.bfloat16)
    second_pass = second_pass.reshape(block_count, local_rows, columns)
    gathered_rows = lax.all_to_all(second_pass, "grp", split_axis=2, concat_axis=1, tiled=True)
    col_count = gathered_rows.shape[2]
    by_piece = gathered_rows.reshape(block_count, 16, 256, col_count)
    mixed_rows = jnp.einsum("ha,nakd->nhkd", hadamard, by_piece, preferred_element_type=jnp.float32)
    mixed_rows = mixed_rows.reshape(block_count, 16 * 256, col_count)
    picked = jax.vmap(pick_rows)(mixed_rows, kept_rows)
    partial_value = jnp.sum(picked, axis=0)
    summed = lax.psum(partial_value, "inner")
    sketch = lax.all_to_all(summed, "grp", split_axis=0, concat_axis=1, tiled=True)
    sketch = sketch * (1.0 / (64.0 * math.sqrt(keep_count)))
    row_base = lax.axis_index("grp") * owned_rows
    global_rows = row_base + jnp.arange(owned_rows, dtype=jnp.int32)

    def reflect(col_index, current):
        column = jnp.where(global_rows >= col_index, current[:, col_index], 0.0)
        is_pivot = (global_rows == col_index).astype(jnp.float32)
        norm_sq, crossed, pivot_row = lax.psum(
            (
                jnp.sum(column * column),
                jnp.dot(column, current, precision=highest),
                jnp.dot(is_pivot, current, precision=highest),
            ),
            "grp",
        )
        pivot_value = pivot_row[col_index]
        head_value = -jnp.where(pivot_value >= 0, 1.0, -1.0) * jnp.sqrt(norm_sq)
        length = 2.0 * (norm_sq - head_value * pivot_value) + epsilon
        projected_row = crossed - head_value * pivot_row
        vector = column - head_value * is_pivot
        return current - vector[:, None] * (2.0 * projected_row / length)[None, :]

    result = lax.fori_loop(0, COLS_DONE, reflect, sketch)
    return result


def solution(mesh):
    return jax.shard_map(
        on_device,
        mesh=mesh,
        in_specs=(P("inner", "grp", None), P("inner", "grp"), P("inner", None)),
        out_specs=P("grp", None),
        check_vma=False,
    )
```

profile of v0, /device:TPU:0, one launch (start us, length us, event | category | flops | bytes accessed | tf_op | source)
XLA Modules:
  0.0 397.2 jit_solution(10092679646443896874)
XLA Ops:
  7.2 2.5 multiply_convert_fusion
  13.1 7.7 %copy.22 = bf16[1,1024,1024]{1,0,2:T(2,128)(2,1)} copy(bf16[1,1024,1024]{2,1,0:T(8,128)(2,1)S(1)} %bitcast.77) | data formatting | bytes 4194304 | tf_op jit(solution)/shard_map/reshape | solution.py:40
  21.4 12.8 %reduce.2 = bf16[1024,1024]{1,0:T(8,128)(2,1)S(1)} reduce(bf16[1024,1,1024]{2,1,0:T(2,128)(2,1)} %bitcast.75, bf16[]{:T(256)} %broadcast.106), dimensions={1}, to_apply=%bitcast.43.reduce_sub_computation | reduce | bytes 4194306
  34.2 2.8 reshape.93
  36.9 6.5 %all-to-all-start = ((bf16[4,2,131072]{2,1,0:T(2,128)(2,1)}), bf16[4,2,131072]{2,1,0:T(2,128)(2,1)S(1)}, u32[]{:S(2)}, u32[]{:S(2)}) async-start(bf16[4,2,131072]{2,1,0:T(2,128)(2,1)} %reshape.93), calls=%async_computation | async-start | bytes 4194304 | tf_op jit(solution)/shard_map/all_to_all | solution.py:41
  43.5 48.1 %all-to-all-done = bf16[4,2,131072]{2,1,0:T(2,128)(2,1)S(1)} async-done(((bf16[4,2,131072]{2,1,0:T(2,128)(2,1)}), bf16[4,2,131072]{2,1,0:T(2,128)(2,1)S(1)}, u32[]{:S(2)}, u32[]{:S(2)}) %all-to-all-start) | async-done | bytes 2097184 | tf_op jit(solution)/shard_map/all_to_all | solution.py:41
  91.6 3.4 reshape.94
  94.9 3.0 copy.29
  97.9 2.6 copy.23
  100.5 2.9 convolution_bitcast_fusion
  103.4 4.4 %copy.25 = f32[1,16,256,256]{3,2,1,0:T(8,128)} copy(f32[1,16,256,256]{3,1,2,0:T(8,128)S(1)} %convolution_bitcast_fusion) | data formatting | bytes 8388608 | tf_op jit(solution)/shard_map/ha,nakd->nhkd/transpose | solution.py:44
  107.8 21.4 %gather_fusion = f32[2048,256]{1,0:T(8,128)S(1)} fusion(f32[1,4096,256]{2,1,0:T(8,128)} %bitcast.74, s32[2048]{0:T(1024)S(1)} %bitcast.73), kind=kCustom, calls=%fused_computation | custom fusion | bytes 4210688 | tf_op jit(solution)/shard_map/vmap(jit(_take))/gather | solution.py:20
  130.8 61.1 %all-reduce.5.cloned.1.call-done = f32[4,512,256]{2,1,0:T(8,128)} async-done(((f32[4,512,256]{2,1,0:T(8,128)}), f32[4,512,256]{2,1,0:T(8,128)}) %all-reduce.5.cloned.1.call-update) | async-done | bytes 2097168 | tf_op jit(solution)/shard_map/psum | solution.py:48
  191.9 4.5 %all-to-all-start.1 = ((f32[4,512,256]{2,1,0:T(8,128)}), f32[4,512,256]{2,1,0:T(8,128)S(1)}, u32[]{:S(2)}, u32[]{:S(2)}) async-start(f32[4,512,256]{2,1,0:T(8,128)} %all-reduce.5.cloned.1.call-done), calls=%async_computation.1 | async-start | bytes 4194304 | tf_op jit(solution)/shard_map/all_to_all | solution.py:49
  196.4 47.1 %all-to-all-done.1 = f32[4,512,256]{2,1,0:T(8,128)S(1)} async-done(((f32[4,512,256]{2,1,0:T(8,128)}), f32[4,512,256]{2,1,0:T(8,128)S(1)}, u32[]{:S(2)}, u32[]{:S(2)}) %all-to-all-start.1) | async-done | bytes 2097184 | tf_op jit(solution)/shard_map/all_to_all | solution.py:49
  247.0 141.5 %while.14 = (s32[]{:T(128)}, f32[512,1024]{0,1:T(8,128)S(1)}, s32[]{:T(128)}, s32[]{:T(128)}, f32[]{:T(128)}, /*index=5*/f32[]{:T(128)}, f32[]{:T(128)}, f32[]{:T(128)}, f32[]{:T(128)}) while((s32[]{:T(128)}, f32[512,1024]{0,1:T(8,128)S(1)}, s32[]{:T(128)}, s32[]{:T(128)}, f32[]{:T(128)}, /*index=5*/f32[]{:T(128)}, f32[]{:T(128)}, ...), condition=%wide.region_6.7_spmd.clone, body=%wide.region_1.6_spmd.clone.sunk | while | flops 13643786 | bytes 8453379 | solution.py:72
  250.5 10.8 %all-reduce.2 = (f32[1024]{0:T(1024)S(1)}, f32[1024]{0:T(1024)S(1)}, f32[]{:T(128)}) all-reduce(f32[1024]{0:T(1024)S(1)} %bitcast.83, f32[1024]{0:T(1024)S(1)} %bitcast.84, f32[]{:T(128)} %get-tuple-element.117), channel_id=1, replica_groups=mesh['grp'=4,'inner'=8] {'grp'}, use_global_device_ids=true, to_apply=%region_5.5 | all-reduce | flops 2049 | bytes 16392 | tf_op jit(solution)/shard_map/while/body/eval_jaxpr/psum | solution.py:57
  268.7 9.9 %all-reduce.2 = (f32[1024]{0:T(1024)S(1)}, f32[1024]{0:T(1024)S(1)}, f32[]{:T(128)}) all-reduce(f32[1024]{0:T(1024)S(1)} %bitcast.83, f32[1024]{0:T(1024)S(1)} %bitcast.84, f32[]{:T(128)} %get-tuple-element.117), channel_id=1, replica_groups=mesh['grp'=4,'inner'=8] {'grp'}, use_global_device_ids=true, to_apply=%region_5.5 | all-reduce | flops 2049 | bytes 16392 | tf_op jit(solution)/shard_map/while/body/eval_jaxpr/psum | solution.py:57
  285.9 10.8 %all-reduce.2 = (f32[1024]{0:T(1024)S(1)}, f32[1024]{0:T(1024)S(1)}, f32[]{:T(128)}) all-reduce(f32[1024]{0:T(1024)S(1)} %bitcast.83, f32[1024]{0:T(1024)S(1)} %bitcast.84, f32[]{:T(128)} %get-tuple-element.117), channel_id=1, replica_groups=mesh['grp'=4,'inner'=8] {'grp'}, use_global_device_ids=true, to_apply=%region_5.5 | all-reduce | flops 2049 | bytes 16392 | tf_op jit(solution)/shard_map/while/body/eval_jaxpr/psum | solution.py:57
  304.0 9.9 %all-reduce.2 = (f32[1024]{0:T(1024)S(1)}, f32[1024]{0:T(1024)S(1)}, f32[]{:T(128)}) all-reduce(f32[1024]{0:T(1024)S(1)} %bitcast.83, f32[1024]{0:T(1024)S(1)} %bitcast.84, f32[]{:T(128)} %get-tuple-element.117), channel_id=1, replica_groups=mesh['grp'=4,'inner'=8] {'grp'}, use_global_device_ids=true, to_apply=%region_5.5 | all-reduce | flops 2049 | bytes 16392 | tf_op jit(solution)/shard_map/while/body/eval_jaxpr/psum | solution.py:57
  321.3 10.8 %all-reduce.2 = (f32[1024]{0:T(1024)S(1)}, f32[1024]{0:T(1024)S(1)}, f32[]{:T(128)}) all-reduce(f32[1024]{0:T(1024)S(1)} %bitcast.83, f32[1024]{0:T(1024)S(1)} %bitcast.84, f32[]{:T(128)} %get-tuple-element.117), channel_id=1, replica_groups=mesh['grp'=4,'inner'=8] {'grp'}, use_global_device_ids=true, to_apply=%region_5.5 | all-reduce | flops 2049 | bytes 16392 | tf_op jit(solution)/shard_map/while/body/eval_jaxpr/psum | solution.py:57
  339.4 9.9 %all-reduce.2 = (f32[1024]{0:T(1024)S(1)}, f32[1024]{0:T(1024)S(1)}, f32[]{:T(128)}) all-reduce(f32[1024]{0:T(1024)S(1)} %bitcast.83, f32[1024]{0:T(1024)S(1)} %bitcast.84, f32[]{:T(128)} %get-tuple-element.117), channel_id=1, replica_groups=mesh['grp'=4,'inner'=8] {'grp'}, use_global_device_ids=true, to_apply=%region_5.5 | all-reduce | flops 2049 | bytes 16392 | tf_op jit(solution)/shard_map/while/body/eval_jaxpr/psum | solution.py:57
  356.7 10.8 %all-reduce.2 = (f32[1024]{0:T(1024)S(1)}, f32[1024]{0:T(1024)S(1)}, f32[]{:T(128)}) all-reduce(f32[1024]{0:T(1024)S(1)} %bitcast.83, f32[1024]{0:T(1024)S(1)} %bitcast.84, f32[]{:T(128)} %get-tuple-element.117), channel_id=1, replica_groups=mesh['grp'=4,'inner'=8] {'grp'}, use_global_device_ids=true, to_apply=%region_5.5 | all-reduce | flops 2049 | bytes 16392 | tf_op jit(solution)/shard_map/while/body/eval_jaxpr/psum | solution.py:57
  374.8 9.9 %all-reduce.2 = (f32[1024]{0:T(1024)S(1)}, f32[1024]{0:T(1024)S(1)}, f32[]{:T(128)}) all-reduce(f32[1024]{0:T(1024)S(1)} %bitcast.83, f32[1024]{0:T(1024)S(1)} %bitcast.84, f32[]{:T(128)} %get-tuple-element.117), channel_id=1, replica_groups=mesh['grp'=4,'inner'=8] {'grp'}, use_global_device_ids=true, to_apply=%region_5.5 | all-reduce | flops 2049 | bytes 16392 | tf_op jit(solution)/shard_map/while/body/eval_jaxpr/psum | solution.py:57
  (105 shorter events, 48.1 us)
Async XLA Ops:
  36.9 6.5 %copy-start = (s32[1,2048]{1,0:T(1,128)S(1)}, s32[1,2048]{1,0:T(1,128)}, u32[]{:S(2)}) copy-start(s32[1,2048]{1,0:T(1,128)} %param.7) | copy-start | bytes 24580
  36.9 54.7 %all-to-all-start = ((bf16[4,2,131072]{2,1,0:T(2,128)(2,1)}), bf16[4,2,131072]{2,1,0:T(2,128)(2,1)S(1)}, u32[]{:S(2)}, u32[]{:S(2)}) async-start(bf16[4,2,131072]{2,1,0:T(2,128)(2,1)} %reshape.93), calls=%async_computation | async-start | bytes 4194304 | tf_op jit(solution)/shard_map/all_to_all | solution.py:41
  43.4 148.5 %all-reduce.5.cloned.1.call-start = ((), (), s32[]{:S(2)}) async-start(), calls=%async_computation.2 | async-start | bytes 4194304 | tf_op jit(solution)/shard_map/psum | solution.py:48
  191.9 51.6 %all-to-all-start.1 = ((f32[4,512,256]{2,1,0:T(8,128)}), f32[4,512,256]{2,1,0:T(8,128)S(1)}, u32[]{:S(2)}, u32[]{:S(2)}) async-start(f32[4,512,256]{2,1,0:T(8,128)} %all-reduce.5.cloned.1.call-done), calls=%async_computation.1 | async-start | bytes 4194304 | tf_op jit(solution)/shard_map/all_to_all | solution.py:49
Sparse Core Ops, SparseCore 0:
  131.0 60.9 all-reduce.4
where the time goes:
time: 398 us; the launch traced here: 397 us
  waiting for transfers between devices  156 us (39%)
  blocking collectives  82.7 us (21%)
  local copies, waits for them, and re-layouts  56 us (14%)
  matrix products  28 us (7%)
  other arithmetic  27.4 us (7%)
  loops' own time  22.4 us (6%)
  between operations  13.5 us (3%)
  starting transfers between devices  11 us (3%)
    psum x8, blocking collectives, reflect(): lax.psum((jnp.sum(column * column), jnp.dot(column, current, precision=hi...  82.7 us
    psum x1, waiting for transfers between devices, on_device(): summed = lax.psum(partial_value, 'inner')  61.1 us
    all_to_all x1, waiting for transfers between devices, on_device(): lax.all_to_all(second_pass, 'grp', split_axis=2, concat_axis=1, tiled=True)  48.1 us
    all_to_all x1, waiting for transfers between devices, on_device(): lax.all_to_all(summed, 'grp', split_axis=0, concat_axis=1, tiled=True)  47.1 us
    another operation x1, loops' own time, on_device(): result = lax.fori_loop(0, COLS_DONE, reflect, sketch)  22.4 us
    gather x2, local copies, waits for them, and re-layouts, pick_rows(): return jnp.take(table_rows, chosen_rows, axis=0)  21.4 us
    dot_general x8, matrix products, reflect(): jnp.dot(column, current, precision=highest)  14.5 us
    unnamed x1, other arithmetic  12.8 us
  transfers between devices with their start and end apart: 3, of which 3 were waited for; matrix products, arithmetic and copies ran while one was open for 0% of the time, Pallas kernels for 0%

commit v1 on v0

--- a/solution.py
+++ b/solution.py
@@ -45,7 +45,9 @@
     mixed_rows = mixed_rows.reshape(block_count, 16 * 256, col_count)
     picked = jax.vmap(pick_rows)(mixed_rows, kept_rows)
     partial_value = jnp.sum(picked, axis=0)
-    summed = lax.psum(partial_value, "inner")
+    summed = partial_value
+    for hop in (1, 2, 4):
+        summed = summed + lax.ppermute(summed, "inner", [(dev, dev ^ hop) for dev in range(8)])
     sketch = lax.all_to_all(summed, "grp", split_axis=0, concat_axis=1, tiled=True)
     sketch = sketch * (1.0 / (64.0 * math.sqrt(keep_count)))
     row_base = lax.axis_index("grp") * owned_rows

time: 398 us -> 422 us (1.060)
  waiting for transfers between devices: 156 us -> 191 us
  between operations: 13.5 us -> 0.13 us
    ppermute x0 -> x3, waiting for transfers between devices: none -> 95.5 us  [on_device(): lax.ppermute(summed, 'inner', [(dev, dev ^ hop) for dev in range(8)])]
    psum x1 -> x0, waiting for transfers between devices: 61.1 us -> none  [on_device(): summed = lax.psum(partial_value, 'inner')]
  transfers between devices with their start and end apart: 3 -> 5, of which waited for: 3 -> 5; matrix products, arithmetic and copies ran while one was open for 0% -> 0% of each run, Pallas kernels for 0% -> 0%
where the time goes in v1:
time: 422 us; the launch traced here: 420 us
  waiting for transfers between devices  191 us (45%)
  blocking collectives  82.7 us (20%)
  local copies, waits for them, and re-layouts  55.6 us (13%)
  other arithmetic  28.4 us (7%)
  matrix products  28 us (7%)
  loops' own time  21.5 us (5%)
  starting transfers between devices  13.5 us (3%)
    ppermute x3, waiting for transfers between devices, on_device(): lax.ppermute(summed, 'inner', [(dev, dev ^ hop) for dev in range(8)])  95.5 us
    psum x8, blocking collectives, reflect(): lax.psum((jnp.sum(column * column), jnp.dot(column, current, precision=hi...  82.7 us
    all_to_all x1, waiting for transfers between devices, on_device(): lax.all_to_all(second_pass, 'grp', split_axis=2, concat_axis=1, tiled=True)  48.1 us
    all_to_all x1, waiting for transfers between devices, on_device(): lax.all_to_all(summed, 'grp', split_axis=0, concat_axis=1, tiled=True)  47 us
    another operation x1, loops' own time, on_device(): result = lax.fori_loop(0, COLS_DONE, reflect, sketch)  21.5 us
    gather x2, local copies, waits for them, and re-layouts, pick_rows(): return jnp.take(table_rows, chosen_rows, axis=0)  21.4 us
    dot_general x8, matrix products, reflect(): jnp.dot(column, current, precision=highest)  14.5 us
    unnamed x1, other arithmetic  12.8 us
  transfers between devices with their start and end apart: 5, of which 5 were waited for; matrix products, arithmetic and copies ran while one was open for 0% of the time, Pallas kernels for 0%

profile of v1, /device:TPU:0, one launch (start us, length us, event | category | flops | bytes accessed | tf_op | source)
XLA Modules:
  0.0 420.3 jit_solution(4067087129136731576)
XLA Ops:
  6.6 7.7 %copy.22 = bf16[1,1024,1024]{1,0,2:T(2,128)(2,1)} copy(bf16[1,1024,1024]{2,1,0:T(8,128)(2,1)S(1)} %bitcast.77) | data formatting | bytes 4194304 | tf_op jit(solution)/shard_map/reshape | solution.py:40
  14.8 12.8 %reduce.2 = bf16[1024,1024]{1,0:T(8,128)(2,1)S(1)} reduce(bf16[1024,1,1024]{2,1,0:T(2,128)(2,1)} %bitcast.75, bf16[]{:T(256)} %broadcast.106), dimensions={1}, to_apply=%bitcast.43.reduce_sub_computation | reduce | bytes 4194306
  27.6 2.8 reshape.93
  30.4 6.5 %all-to-all-start = ((bf16[4,2,131072]{2,1,0:T(2,128)(2,1)}), bf16[4,2,131072]{2,1,0:T(2,128)(2,1)S(1)}, u32[]{:S(2)}, u32[]{:S(2)}) async-start(bf16[4,2,131072]{2,1,0:T(2,128)(2,1)} %reshape.93), calls=%async_computation | async-start | bytes 4194304 | tf_op jit(solution)/shard_map/all_to_all | solution.py:41
  37.0 48.1 %all-to-all-done = bf16[4,2,131072]{2,1,0:T(2,128)(2,1)S(1)} async-done(((bf16[4,2,131072]{2,1,0:T(2,128)(2,1)}), bf16[4,2,131072]{2,1,0:T(2,128)(2,1)S(1)}, u32[]{:S(2)}, u32[]{:S(2)}) %all-to-all-start) | async-done | bytes 2097184 | tf_op jit(solution)/shard_map/all_to_all | solution.py:41
  85.1 3.4 reshape.94
  88.4 3.0 copy.29
  94.0 2.9 convolution_bitcast_fusion
  96.9 4.4 %copy.25 = f32[1,16,256,256]{3,2,1,0:T(8,128)} copy(f32[1,16,256,256]{3,1,2,0:T(8,128)S(1)} %convolution_bitcast_fusion) | data formatting | bytes 8388608 | tf_op jit(solution)/shard_map/ha,nakd->nhkd/transpose | solution.py:44
  101.3 21.4 %gather_fusion = f32[2048,256]{1,0:T(8,128)S(1)} fusion(f32[1,4096,256]{2,1,0:T(8,128)} %bitcast.74, s32[2048]{0:T(1024)S(1)} %bitcast.73), kind=kCustom, calls=%fused_computation | custom fusion | bytes 4210688 | tf_op jit(solution)/shard_map/vmap(jit(_take))/gather | solution.py:20
  123.1 4.1 collective-permute-done
  129.3 46.1 %collective-permute-done.1 = f32[2048,256]{1,0:T(8,128)S(1)} collective-permute-done((f32[2048,256]{1,0:T(8,128)S(1)}, f32[2048,256]{1,0:T(8,128)S(1)}, u32[]{:S(2)}, u32[]{:S(2)}) %collective-permute-start.1) | collective-permute-done | bytes 2097184 | tf_op jit(solution)/shard_map/ppermute | solution.py:50
  177.3 45.2 %collective-permute-done.2 = f32[2048,256]{1,0:T(8,128)S(1)} collective-permute-done((f32[2048,256]{1,0:T(8,128)S(1)}, f32[2048,256]{1,0:T(8,128)S(1)}, u32[]{:S(2)}, u32[]{:S(2)}) %collective-permute-start.2) | collective-permute-done | bytes 2097184 | tf_op jit(solution)/shard_map/ppermute | solution.py:50
  224.1 3.6 all-to-all-start.1
  227.8 47.0 %all-to-all-done.1 = f32[4,512,256]{2,1,0:T(8,128)S(1)} async-done(((f32[4,512,256]{2,1,0:T(8,128)}), f32[4,512,256]{2,1,0:T(8,128)S(1)}, u32[]{:S(2)}, u32[]{:S(2)}) %all-to-all-start.1) | async-done | bytes 2097184 | tf_op jit(solution)/shard_map/all_to_all | solution.py:51
  278.2 140.2 %while.14 = (s32[]{:T(128)}, f32[512,1024]{0,1:T(8,128)S(1)}, s32[]{:T(128)}, s32[]{:T(128)}, f32[]{:T(128)}, /*index=5*/f32[]{:T(128)}, f32[]{:T(128)}, f32[]{:T(128)}, f32[]{:T(128)}) while((s32[]{:T(128)}, f32[512,1024]{0,1:T(8,128)S(1)}, s32[]{:T(128)}, s32[]{:T(128)}, f32[]{:T(128)}, /*index=5*/f32[]{:T(128)}, f32[]{:T(128)}, ...), condition=%wide.region_5.6_spmd.clone, body=%wide.region_0.5_spmd.clone.sunk | while | flops 13643786 | bytes 8453379 | solution.py:74
  281.8 10.8 %all-reduce.2 = (f32[1024]{0:T(1024)S(1)}, f32[1024]{0:T(1024)S(1)}, f32[]{:T(128)}) all-reduce(f32[1024]{0:T(1024)S(1)} %bitcast.82, f32[1024]{0:T(1024)S(1)} %bitcast.83, f32[]{:T(128)} %get-tuple-element.117), channel_id=1, replica_groups=mesh['grp'=4,'inner'=8] {'grp'}, use_global_device_ids=true, to_apply=%region_4.4 | all-reduce | flops 2049 | bytes 16392 | tf_op jit(solution)/shard_map/while/body/eval_jaxpr/psum | solution.py:59
  299.7 9.9 %all-reduce.2 = (f32[1024]{0:T(1024)S(1)}, f32[1024]{0:T(1024)S(1)}, f32[]{:T(128)}) all-reduce(f32[1024]{0:T(1024)S(1)} %bitcast.82, f32[1024]{0:T(1024)S(1)} %bitcast.83, f32[]{:T(128)} %get-tuple-element.117), channel_id=1, replica_groups=mesh['grp'=4,'inner'=8] {'grp'}, use_global_device_ids=true, to_apply=%region_4.4 | all-reduce | flops 2049 | bytes 16392 | tf_op jit(solution)/shard_map/while/body/eval_jaxpr/psum | solution.py:59
  316.8 10.8 %all-reduce.2 = (f32[1024]{0:T(1024)S(1)}, f32[1024]{0:T(1024)S(1)}, f32[]{:T(128)}) all-reduce(f32[1024]{0:T(1024)S(1)} %bitcast.82, f32[1024]{0:T(1024)S(1)} %bitcast.83, f32[]{:T(128)} %get-tuple-element.117), channel_id=1, replica_groups=mesh['grp'=4,'inner'=8] {'grp'}, use_global_device_ids=true, to_apply=%region_4.4 | all-reduce | flops 2049 | bytes 16392 | tf_op jit(solution)/shard_map/while/body/eval_jaxpr/psum | solution.py:59
  334.8 9.9 %all-reduce.2 = (f32[1024]{0:T(1024)S(1)}, f32[1024]{0:T(1024)S(1)}, f32[]{:T(128)}) all-reduce(f32[1024]{0:T(1024)S(1)} %bitcast.82, f32[1024]{0:T(1024)S(1)} %bitcast.83, f32[]{:T(128)} %get-tuple-element.117), channel_id=1, replica_groups=mesh['grp'=4,'inner'=8] {'grp'}, use_global_device_ids=true, to_apply=%region_4.4 | all-reduce | flops 2049 | bytes 16392 | tf_op jit(solution)/shard_map/while/body/eval_jaxpr/psum | solution.py:59
  351.9 10.8 %all-reduce.2 = (f32[1024]{0:T(1024)S(1)}, f32[1024]{0:T(1024)S(1)}, f32[]{:T(128)}) all-reduce(f32[1024]{0:T(1024)S(1)} %bitcast.82, f32[1024]{0:T(1024)S(1)} %bitcast.83, f32[]{:T(128)} %get-tuple-element.117), channel_id=1, replica_groups=mesh['grp'=4,'inner'=8] {'grp'}, use_global_device_ids=true, to_apply=%region_4.4 | all-reduce | flops 2049 | bytes 16392 | tf_op jit(solution)/shard_map/while/body/eval_jaxpr/psum | solution.py:59
  369.9 9.9 %all-reduce.2 = (f32[1024]{0:T(1024)S(1)}, f32[1024]{0:T(1024)S(1)}, f32[]{:T(128)}) all-reduce(f32[1024]{0:T(1024)S(1)} %bitcast.82, f32[1024]{0:T(1024)S(1)} %bitcast.83, f32[]{:T(128)} %get-tuple-element.117), channel_id=1, replica_groups=mesh['grp'=4,'inner'=8] {'grp'}, use_global_device_ids=true, to_apply=%region_4.4 | all-reduce | flops 2049 | bytes 16392 | tf_op jit(solution)/shard_map/while/body/eval_jaxpr/psum | solution.py:59
  386.9 11.0 %all-reduce.2 = (f32[1024]{0:T(1024)S(1)}, f32[1024]{0:T(1024)S(1)}, f32[]{:T(128)}) all-reduce(f32[1024]{0:T(1024)S(1)} %bitcast.82, f32[1024]{0:T(1024)S(1)} %bitcast.83, f32[]{:T(128)} %get-tuple-element.117), channel_id=1, replica_groups=mesh['grp'=4,'inner'=8] {'grp'}, use_global_device_ids=true, to_apply=%region_4.4 | all-reduce | flops 2049 | bytes 16392 | tf_op jit(solution)/shard_map/while/body/eval_jaxpr/psum | solution.py:59
  405.1 9.7 %all-reduce.2 = (f32[1024]{0:T(1024)S(1)}, f32[1024]{0:T(1024)S(1)}, f32[]{:T(128)}) all-reduce(f32[1024]{0:T(1024)S(1)} %bitcast.82, f32[1024]{0:T(1024)S(1)} %bitcast.83, f32[]{:T(128)} %get-tuple-element.117), channel_id=1, replica_groups=mesh['grp'=4,'inner'=8] {'grp'}, use_global_device_ids=true, to_apply=%region_4.4 | all-reduce | flops 2049 | bytes 16392 | tf_op jit(solution)/shard_map/while/body/eval_jaxpr/psum | solution.py:59
  (111 shorter events, 57.1 us)
Async XLA Ops:
  30.4 6.5 %copy-start = (s32[1,2048]{1,0:T(1,128)S(1)}, s32[1,2048]{1,0:T(1,128)}, u32[]{:S(2)}) copy-start(s32[1,2048]{1,0:T(1,128)} %param.7) | copy-start | bytes 24580
  30.4 54.7 %all-to-all-start = ((bf16[4,2,131072]{2,1,0:T(2,128)(2,1)}), bf16[4,2,131072]{2,1,0:T(2,128)(2,1)S(1)}, u32[]{:S(2)}, u32[]{:S(2)}) async-start(bf16[4,2,131072]{2,1,0:T(2,128)(2,1)} %reshape.93), calls=%async_computation | async-start | bytes 4194304 | tf_op jit(solution)/shard_map/all_to_all | solution.py:41
  123.0 4.2 %collective-permute-start = (f32[2048,256]{1,0:T(8,128)S(1)}, f32[2048,256]{1,0:T(8,128)S(1)}, u32[]{:S(2)}, u32[]{:S(2)}) collective-permute-start(f32[2048,256]{1,0:T(8,128)S(1)} %broadcast_select_fusion.2), channel_id=1, source_target_pairs={{0,1},{1,0},{2,3},{3,2},{4,5},{5,4},{6,7},{7,6},{8,9},{9,8},{10,11... | collective-permute-start | bytes 6291464 | tf_op jit(solution)/shard_map/ppermute | solution.py:50
  127.7 47.7 %collective-permute-start.1 = (f32[2048,256]{1,0:T(8,128)S(1)}, f32[2048,256]{1,0:T(8,128)S(1)}, u32[]{:S(2)}, u32[]{:S(2)}) collective-permute-start(f32[2048,256]{1,0:T(8,128)S(1)} %fusion.43), channel_id=1, source_target_pairs={{0,2},{1,3},{2,0},{3,1},{4,6},{5,7},{6,4},{7,5},{8,10},{9,11},{10,... | collective-permute-start | bytes 6291464 | tf_op jit(solution)/shard_map/ppermute | solution.py:50
  175.7 46.9 %collective-permute-start.2 = (f32[2048,256]{1,0:T(8,128)S(1)}, f32[2048,256]{1,0:T(8,128)S(1)}, u32[]{:S(2)}, u32[]{:S(2)}) collective-permute-start(f32[2048,256]{1,0:T(8,128)S(1)} %add.85), channel_id=1, source_target_pairs={{0,4},{1,5},{2,6},{3,7},{4,0},{5,1},{6,2},{7,3},{8,12},{9,13},{10,... | collective-permute-start | bytes 6291464 | tf_op jit(solution)/shard_map/ppermute | solution.py:50
  224.1 50.6 %all-to-all-start.1 = ((f32[4,512,256]{2,1,0:T(8,128)}), f32[4,512,256]{2,1,0:T(8,128)S(1)}, u32[]{:S(2)}, u32[]{:S(2)}) async-start(f32[4,512,256]{2,1,0:T(8,128)} %bitcast.17), calls=%async_computation.1 | async-start | bytes 4194304 | tf_op jit(solution)/shard_map/all_to_all | solution.py:51
